TPU v7x, 32 devices: a whole 2x2x4 slice. The times are simulated.
32 devices in a mesh: pa: 4 (over y, core), pb: 8 (over z, x).
Axes of the slice: x: 2, y: 2, z: 4, core: 2. Of those that a mesh axis runs over, the one named last changes fastest.
Arguments:
- excitons: bfloat16 [2, 512, 1024], P(None, 'pa', 'pb'), may hold values from -6 to 6
- screened: bfloat16 [16384, 16384], P('pa', 'pb'), may hold values from -0.25 to 0.25
- phi_val: bfloat16 [16384, 512], P('pa'), may hold values from -0.25 to 0.25
- phi_con: bfloat16 [16384, 1024], P('pb'), may hold values from -0.1875 to 0.1875
Outputs:
- kernel_out: bfloat16 [2, 512, 1024], P(None, 'pa', 'pb')
All inputs are finite; a program needn't handle non-finite values.
Results may differ from a plain program's by a relative error of at most 0.0057.
Values may be sent and summed in bfloat16 or wider, within the bound.
No kernel may reach another device: no remote copies, remote signals or barrier semaphores. Data moves between devices by JAX's collectives and lax.ppermute only.
A program may use at most 192 MiB of HBM per device.

v0:
```python
import jax
import jax.numpy as jnp
from jax import lax
from jax.sharding import PartitionSpec as P


def local(excitons, screened, phi_val, phi_con):
    high = lax.Precision.HIGHEST
    val_rows = lax.all_gather(excitons, "pb", axis=2, tiled=True)
    half_exp = jnp.einsum(
        "evc,qc->evq",
        lax.all_gather(val_rows, "pa", axis=1, tiled=True),
        phi_con,
        preferred_element_type=jnp.float32,
    ).astype(jnp.bfloat16)
    expanded = jnp.einsum("pv,evq->epq", phi_val, half_exp, preferred_element_type=jnp.float32)
    weighted = (screened.astype(jnp.float32)[None] * expanded).astype(jnp.bfloat16)
    partial_value = jnp.einsum("pv,epq->evq", phi_val, weighted, preferred_element_type=jnp.float32)
    con_float = phi_con.astype(jnp.float32)
    terms = jnp.einsum("evq,qc->evc", partial_value, con_float, precision=high)
    columns = lax.psum_scatter(terms, "pb", scatter_dimension=2, tiled=True)
    result = lax.psum_scatter(columns, "pa", scatter_dimension=1, tiled=True)
    return result.astype(jnp.bfloat16)


def solution(mesh):
    placed = (P(None, "pa", "pb"), P("pa", "pb"), P("pa", None), P("pb", None))
    return jax.shard_map(
        local, mesh=mesh, in_specs=placed, out_specs=P(None, "pa", "pb"), check_vma=False
    )
```

profile of v0, /device:TPU:0, one launch (start us, length us, event | category | flops | bytes accessed | tf_op | source)
XLA Modules:
  0.0 260.3 jit_solution(2940196024953835160)
XLA Ops:
  6.5 0.0 all-gather.2.cloned.1.call-start
  6.5 31.1 %all_gather.6 = bf16[2,128,1024]{2,1,0:T(8,128)(2,1)} all-gather(bf16[2,128,128]{2,1,0:T(8,128)(2,1)} %param.4), channel_id=1, replica_groups=mesh['pa'=4,'pb'=8] {'pb'}, dimensions={2}, use_global_device_ids=true | all-gather | bytes 589824 | tf_op jit(solution)/shard_map/all_gather | solution.py:9
  37.6 0.0 all-gather.2.cloned.1.call-update
  37.6 0.0 reduce-scatter.3.cloned.1.call-start
  37.7 18.8 %convert_element_type.13 = f32[4096,2048]{1,0:T(8,128)} convert(bf16[4096,2048]{1,0:T(8,128)(2,1)} %param.5) | non-fusion elementwise | flops 8388608 | bytes 50331648 | tf_op jit(solution)/shard_map/convert_element_type | solution.py:17
  56.5 2.3 all-gather.2.cloned.1.call-done
  58.8 9.3 %fusion.11 = bf16[2,512,2048]{2,1,0:T(8,128)(2,1)} fusion(bf16[2,512,1024]{2,1,0:T(8,128)(2,1)} %all-gather.2.cloned.1.call-done, bf16[2048,1024]{1,0:T(8,128)(2,1)} %param.7), kind=kOutput, calls=%fused_computation.9 | convolution fusion | flops 4294967296 | bytes 10485760 | tf_op jit(solution)/shard_map/evc,qc->evq/dot_general | solution.py:10
  68.1 33.7 %fusion.26 = bf16[2,4096,2048]{2,1,0:T(8,128)(2,1)} fusion(f32[4096,2048]{1,0:T(8,128)} %convert_element_type.13, bf16[4096,512]{1,0:T(8,128)(2,1)} %param.6, bf16[2,512,2048]{2,1,0:T(8,128)(2,1)} %fusion.11), kind=kOutput, calls=%fused_computation.1.clone.clone.1 | convolution fusion | flops 17213423616 | bytes 75497472 | tf_op jit(solution)/shard_map/pv,evq->epq/dot_general | solution.py:16
  101.8 0.0 copy-start
  101.8 22.9 %fusion.1 = f32[2,2048,512]{1,2,0:T(8,128)S(1)} fusion(bf16[4096,512]{1,0:T(8,128)(2,1)} %param.6, bf16[2,4096,2048]{2,1,0:T(8,128)(2,1)} %fusion.26), kind=kOutput, calls=%fused_computation.2 | convolution fusion | flops 17179869184 | bytes 46137344 | tf_op jit(solution)/shard_map/pv,epq->evq/dot_general | solution.py:18
  124.7 0.0 copy-done
  124.7 14.9 %fusion.4 = f32[2,512,1024]{2,1,0:T(8,128)} fusion(f32[2,2048,512]{1,2,0:T(8,128)S(1)} %fusion.1, bf16[2048,1024]{1,0:T(8,128)(2,1)S(1)} %copy-done), kind=kOutput, calls=%fused_computation.4 | convolution fusion | flops 25769803776 | bytes 16777216 | tf_op jit(solution)/shard_map/evq,qc->evc/dot_general | solution.py:20
  139.6 0.0 reduce-scatter.3.cloned.1.call-update
  139.6 0.0 reduce-scatter.5.cloned.1.call-start
  139.6 88.8 %reduce-scatter.3.cloned.1.call-done = f32[2,512,128]{2,1,0:T(8,128)} async-done(((f32[2,512,1024]{2,1,0:T(8,128)}), f32[2,512,128]{2,1,0:T(8,128)}) %reduce-scatter.3.cloned.1.call-update) | async-done | bytes 524304 | tf_op jit(solution)/shard_map/reduce_scatter | solution.py:21
  228.4 0.0 reduce-scatter.5.cloned.1.call-update
  228.4 23.8 %reduce-scatter.5.cloned.1.call-done = f32[2,128,128]{2,1,0:T(8,128)} async-done(((f32[2,512,128]{2,1,0:T(8,128)}), f32[2,128,128]{2,1,0:T(8,128)}) %reduce-scatter.5.cloned.1.call-update) | async-done | bytes 131088 | tf_op jit(solution)/shard_map/reduce_scatter | solution.py:22
  252.3 1.5 convert_element_type.16
Async XLA Ops:
  6.5 52.3 %all-gather.2.cloned.1.call-start = ((), (), s32[]{:S(2)}) async-start(), calls=%async_computation.2 | async-start | bytes 2621440 | tf_op jit(solution)/shard_map/all_gather | solution.py:12
  37.6 190.8 %reduce-scatter.3.cloned.1.call-start = ((), (), s32[]{:S(2)}) async-start(), calls=%async_computation.3 | async-start | bytes 4718592 | tf_op jit(solution)/shard_map/reduce_scatter | solution.py:21
  101.8 22.9 %copy-start = (bf16[2048,1024]{1,0:T(8,128)(2,1)S(1)}, bf16[2048,1024]{1,0:T(8,128)(2,1)}, u32[]{:S(2)}) copy-start(bf16[2048,1024]{1,0:T(8,128)(2,1)} %param.7) | copy-start | bytes 12582916
  139.6 112.7 %reduce-scatter.5.cloned.1.call-start = ((), (), s32[]{:S(2)}) async-start(), calls=%async_computation.4 | async-start | bytes 655360 | tf_op jit(solution)/shard_map/reduce_scatter | solution.py:22
Sparse Core Ops, SparseCore 0:
  37.8 20.9 all-gather.1
  139.7 88.6 reduce-scatter.2
  230.9 21.3 reduce-scatter.4
where the time goes:
time: 261 us; the launch traced here: 260 us
  waiting for transfers between devices  115 us (44%)
  matrix products  80.8 us (31%)
  blocking collectives  31.1 us (12%)
  other arithmetic  20.4 us (8%)
  between operations  13.1 us (5%)
    reduce_scatter x1, waiting for transfers between devices, local(): columns = lax.psum_scatter(terms, 'pb', scatter_dimension=2, tiled=True)  88.8 us
    dot_general x1, matrix products, local(): jnp.einsum('pv,evq->epq', phi_val, half_exp, preferred_element_type=jnp.f...  33.7 us
    all_gather x1, blocking collectives, local(): val_rows = lax.all_gather(excitons, 'pb', axis=2, tiled=True)  31.1 us
    reduce_scatter x1, waiting for transfers between devices, local(): result = lax.psum_scatter(columns, 'pa', scatter_dimension=1, tiled=True)  23.8 us
    dot_general x1, matrix products, local(): jnp.einsum('pv,epq->evq', phi_val, weighted, preferred_element_type=jnp.f...  22.9 us
    convert_element_type x1, other arithmetic, local(): screened.astype(jnp.float32)[None] * expanded  18.8 us
    dot_general x1, matrix products, local(): terms = jnp.einsum('evq,qc->evc', partial_value, con_float, precision=high)  14.9 us
    dot_general x1, matrix products, local(): jnp.einsum('evc,qc->evq', lax.all_gather(val_rows, 'pa', axis=1, tiled=Tr...  9.34 us
  transfers between devices with their start and end apart: 3, of which 3 were waited for; matrix products, arithmetic and copies ran while one was open for 7% of the time, Pallas kernels for 0%

commit v1 on v0

--- a/solution.py
+++ b/solution.py
@@ -4,14 +4,31 @@
 from jax.sharding import PartitionSpec as P
 
 
+def work_both_ways(array, axis, dim, make, out_dim):
+    ways, here, lap = (lax.axis_size(axis), lax.axis_index(axis), array.shape[dim])
+    earlier, later = ([], [])
+    going_up = going_down = array
+    for far in range(ways // 2 + 1):
+        earlier.append(make(going_up, (here - far) % ways * lap))
+        if 0 < far < ways - ways // 2:
+            later.append(make(going_down, (here + far) % ways * lap))
+        going_up = lax.ppermute(going_up, axis, [(d, (d + 1) % ways) for d in range(ways)])
+        going_down = lax.ppermute(going_down, axis, [(d, (d - 1) % ways) for d in range(ways)])
+    line = jnp.concatenate([*earlier[::-1], *later], axis=out_dim)
+    return jnp.roll(line, (here - ways // 2) * earlier[0].shape[out_dim], axis=out_dim)
+
+
 def local(excitons, screened, phi_val, phi_con):
     high = lax.Precision.HIGHEST
     val_rows = lax.all_gather(excitons, "pb", axis=2, tiled=True)
-    half_exp = jnp.einsum(
-        "evc,qc->evq",
-        lax.all_gather(val_rows, "pa", axis=1, tiled=True),
-        phi_con,
-        preferred_element_type=jnp.float32,
+    half_exp = work_both_ways(
+        val_rows,
+        "pa",
+        1,
+        lambda part, start: jnp.einsum(
+            "evc,qc->evq", part, phi_con, preferred_element_type=jnp.float32
+        ),
+        1,
     ).astype(jnp.bfloat16)
     expanded = jnp.einsum("pv,evq->epq", phi_val, half_exp, preferred_element_type=jnp.float32)
     weighted = (screened.astype(jnp.float32)[None] * expanded).astype(jnp.bfloat16)

time: 261 us -> 274 us (1.050)
  waiting for transfers between devices: 115 us -> 120 us
  local copies, waits for them, and re-layouts: 0.01 us -> 4.18 us
  matrix products: 80.8 us -> 84.7 us
    ppermute x0 -> x3, waiting for transfers between devices: none -> 8.61 us  [the longest x2 8.61 us: work_both_ways(): lax.ppermute(going_up, axis, [(d, (d + 1) % ways) for d in range(ways)])]
    dot_general x1 -> x4, matrix products: 9.34 us -> 13.5 us  [local(): jnp.einsum('evc,qc->evq', part, phi_con, preferred_element_type=jnp.float32)]
    unnamed x2 -> x7, local copies, waits for them, and re-layouts: 0.01 us -> 3.1 us
  transfers between devices with their start and end apart: 3 -> 5, of which waited for: 3 -> 3; matrix products, arithmetic and copies ran while one was open for 7% -> 11% of each run, Pallas kernels for 0% -> 0%
where the time goes in v1:
time: 274 us
  waiting for transfers between devices  120 us (44%)
  matrix products  84.7 us (31%)
  blocking collectives  29.8 us (11%)
  other arithmetic  20.2 us (7%)
  between operations  13.4 us (5%)
  local copies, waits for them, and re-layouts  4.18 us (2%)
    reduce_scatter x1, waiting for transfers between devices, local(): columns = lax.psum_scatter(terms, 'pb', scatter_dimension=2, tiled=True)  87.6 us
    dot_general x1, matrix products, local(): jnp.einsum('pv,evq->epq', phi_val, half_exp, preferred_element_type=jnp.f...  33.6 us
    all_gather x1, blocking collectives, local(): val_rows = lax.all_gather(excitons, 'pb', axis=2, tiled=True)  29.8 us
    reduce_scatter x1, waiting for transfers between devices, local(): result = lax.psum_scatter(columns, 'pa', scatter_dimension=1, tiled=True)  23.8 us
    dot_general x1, matrix products, local(): jnp.einsum('pv,epq->evq', phi_val, weighted, preferred_element_type=jnp.f...  22.9 us
    convert_element_type x1, other arithmetic, local(): screened.astype(jnp.float32)[None] * expanded  18.7 us
    dot_general x1, matrix products, local(): terms = jnp.einsum('evq,qc->evc', partial_value, con_float, precision=high)  14.7 us
    dot_general x4, matrix products, local(): jnp.einsum('evc,qc->evq', part, phi_con, preferred_element_type=jnp.float32)  13.5 us
  transfers between devices with their start and end apart: 5, of which 3 were waited for; matrix products, arithmetic and copies ran while one was open for 11% of the time, Pallas kernels for 0%

profile of v1, /device:TPU:0, one launch (start us, length us, event | category | flops | bytes accessed | tf_op | source)
XLA Modules:
  0.0 274.2 jit_solution(13711400594753581959)
XLA Ops:
  6.5 0.0 reduce-scatter.3.cloned.1.call-start
  6.5 29.8 %all_gather.3 = bf16[2,128,1024]{2,1,0:T(8,128)(2,1)S(1)} all-gather(bf16[2,128,128]{2,1,0:T(8,128)(2,1)} %param.4), channel_id=1, replica_groups=mesh['pa'=4,'pb'=8] {'pb'}, dimensions={2}, use_global_device_ids=true | all-gather | bytes 589824 | tf_op jit(solution)/shard_map/all_gather | solution.py:23
  36.3 0.0 collective-permute-start
  36.3 8.6 %collective-permute-done = bf16[2,128,1024]{2,1,0:T(8,128)(2,1)S(1)} collective-permute-done((bf16[2,128,1024]{2,1,0:T(8,128)(2,1)S(1)}, bf16[2,128,1024]{2,1,0:T(8,128)(2,1)S(1)}, u32[]{:S(2)}, u32[]{:S(2)}) %collective-permute-start) | collective-permute-done | bytes 524320 | tf_op jit(solution)/shard_map/ppermute | solution.py:15
  44.9 0.0 collective-permute-start.1
  44.9 1.7 collective-permute-start.2
  46.7 18.7 %convert_element_type.13 = f32[4096,2048]{1,0:T(8,128)} convert(bf16[4096,2048]{1,0:T(8,128)(2,1)} %param.5) | non-fusion elementwise | flops 8388608 | bytes 50331648 | tf_op jit(solution)/shard_map/convert_element_type | solution.py:34
  65.4 0.0 copy-start
  65.4 0.0 collective-permute-done.1
  65.4 4.6 %constant_dynamic-update-slice_fusion.7 = (bf16[2,1024,2048]{2,1,0:T(8,128)(2,1)}, bf16[2,128,2048]{2,1,0:T(8,128)(2,1)S(1)}) fusion(bf16[2,128,1024]{2,1,0:T(8,128)(2,1)S(1)} %collective-permute-done.1, bf16[2048,1024]{1,0:T(8,128)(2,1)} %param.7), kind=kOutput, calls=%fused_computation.25 | convolution fusion | flops 1073741824 | bytes 6815744 | tf_op jit(solution)/shard_map/evc,qc->evq/dot_general | solution.py:28
  69.9 4.4 %constant_dynamic-update-slice_fusion.6 = (bf16[2,1024,2048]{2,1,0:T(8,128)(2,1)}, bf16[2,128,2048]{2,1,0:T(8,128)(2,1)S(1)}) fusion(bf16[2,1024,2048]{2,1,0:T(8,128)(2,1)} %get-tuple-element.5, bf16[2,128,1024]{2,1,0:T(8,128)(2,1)S(1)} %collective-permute-done, bf16[2048,1024]{1,0:T(8,128)(2,1)} %param.7), kind=kOutput, calls=%fused_computation.24 | convolution fusion | flops 1073741824 | bytes 6815744 | tf_op jit(solution)/shard_map/evc,qc->evq/dot_general | solution.py:28
  74.4 0.0 copy-done
  74.4 2.3 constant_dynamic-update-slice_fusion.5
  76.6 0.0 collective-permute-done.2
  76.6 2.2 constant_dynamic-update-slice_fusion.4
  78.9 1.0 constant_dynamic-update-slice_fusion.3
  79.9 1.0 constant_dynamic-update-slice_fusion.2
  80.9 1.0 constant_dynamic-update-slice_fusion.1
  82.0 1.1 constant_dynamic-update-slice_fusion
  83.0 33.6 %fusion.31 = bf16[2,4096,2048]{2,1,0:T(8,128)(2,1)} fusion(f32[4096,2048]{1,0:T(8,128)} %convert_element_type.13, bf16[2,1024,2048]{2,1,0:T(8,128)(2,1)} %constant_dynamic-update-slice_fusion, s32[]{:T(128)S(6)} %select_n.14, bf16[4096,512]{1,0:T(8,128)(2,1)} %param.6), kind=kOutput, calls=%fused_computation.1.clone.clone.1 | convolution fusion | flops 17213423616 | bytes 75497472 | tf_op jit(solution)/shard_map/pv,evq->epq/dot_general | solution.py:33
  116.7 0.0 copy-start.1
  116.7 22.9 %fusion.1 = f32[2,2048,512]{1,2,0:T(8,128)S(1)} fusion(bf16[4096,512]{1,0:T(8,128)(2,1)} %param.6, bf16[2,4096,2048]{2,1,0:T(8,128)(2,1)} %fusion.31), kind=kOutput, calls=%fused_computation.2 | convolution fusion | flops 17179869184 | bytes 46137344 | tf_op jit(solution)/shard_map/pv,epq->evq/dot_general | solution.py:35
  139.5 0.0 copy-done.1
  139.5 14.7 %fusion.4 = f32[2,512,1024]{2,1,0:T(8,128)} fusion(f32[2,2048,512]{1,2,0:T(8,128)S(1)} %fusion.1, bf16[2048,1024]{1,0:T(8,128)(2,1)S(1)} %copy-done.1), kind=kOutput, calls=%fused_computation.4 | convolution fusion | flops 25769803776 | bytes 16777216 | tf_op jit(solution)/shard_map/evq,qc->evc/dot_general | solution.py:37
  154.3 0.0 reduce-scatter.3.cloned.1.call-update
  154.3 0.0 reduce-scatter.5.cloned.1.call-start
  154.4 87.6 %reduce-scatter.3.cloned.1.call-done = f32[2,512,128]{2,1,0:T(8,128)} async-done(((f32[2,512,1024]{2,1,0:T(8,128)}), f32[2,512,128]{2,1,0:T(8,128)}) %reduce-scatter.3.cloned.1.call-update) | async-done | bytes 524304 | tf_op jit(solution)/shard_map/reduce_scatter | solution.py:38
  242.0 0.0 reduce-scatter.5.cloned.1.call-update
  242.0 23.8 %reduce-scatter.5.cloned.1.call-done = f32[2,128,128]{2,1,0:T(8,128)} async-done(((f32[2,512,128]{2,1,0:T(8,128)}), f32[2,128,128]{2,1,0:T(8,128)}) %reduce-scatter.5.cloned.1.call-update) | async-done | bytes 131088 | tf_op jit(solution)/shard_map/reduce_scatter | solution.py:39
  265.8 1.5 convert_element_type.16
Async XLA Ops:
  6.5 235.4 %reduce-scatter.3.cloned.1.call-start = ((), (), s32[]{:S(2)}) async-start(), calls=%async_computation.2 | async-start | bytes 4718592 | tf_op jit(solution)/shard_map/reduce_scatter | solution.py:38
  36.3 8.6 %collective-permute-start = (bf16[2,128,1024]{2,1,0:T(8,128)(2,1)S(1)}, bf16[2,128,1024]{2,1,0:T(8,128)(2,1)S(1)}, u32[]{:S(2)}, u32[]{:S(2)}) collective-permute-start(bf16[2,128,1024]{2,1,0:T(8,128)(2,1)S(1)} %all_gather.3), channel_id=1, source_target_pairs={{0,8},{8,16},{16,24},{24,0},{1,9},{9,17},{17,25},{25,1},{2,10},{10... | collective-permute-start | bytes 1572872 | tf_op jit(solution)/shard_map/ppermute | solution.py:15
  44.9 20.4 %collective-permute-start.1 = (bf16[2,128,1024]{2,1,0:T(8,128)(2,1)S(1)}, bf16[2,128,1024]{2,1,0:T(8,128)(2,1)S(1)}, u32[]{:S(2)}, u32[]{:S(2)}) collective-permute-start(bf16[2,128,1024]{2,1,0:T(8,128)(2,1)S(1)} %collective-permute-done), channel_id=1, source_target_pairs={{0,8},{8,16},{16,24},{24,0},{1,9},{9,17},{17,25},{25,1},{2,10},{10... | collective-permute-start | bytes 1572872 | tf_op jit(solution)/shard_map/ppermute | solution.py:15
  44.9 31.7 %collective-permute-start.2 = (bf16[2,128,1024]{2,1,0:T(8,128)(2,1)S(1)}, bf16[2,128,1024]{2,1,0:T(8,128)(2,1)S(1)}, u32[]{:S(2)}, u32[]{:S(2)}) collective-permute-start(bf16[2,128,1024]{2,1,0:T(8,128)(2,1)S(1)} %all_gather.3), channel_id=1, source_target_pairs={{0,24},{8,0},{16,8},{24,16},{1,25},{9,1},{17,9},{25,17},{2,26},{10... | collective-permute-start | bytes 1572872 | tf_op jit(solution)/shard_map/ppermute | solution.py:16
  65.4 9.0 %copy-start = (bf16[2048,1024]{1,0:T(8,128)(2,1)S(1)}, bf16[2048,1024]{1,0:T(8,128)(2,1)}, u32[]{:S(2)}) copy-start(bf16[2048,1024]{1,0:T(8,128)(2,1)} %param.7) | copy-start | bytes 12582916
  116.7 22.9 %copy-start.1 = (bf16[2048,1024]{1,0:T(8,128)(2,1)S(1)}, bf16[2048,1024]{1,0:T(8,128)(2,1)}, u32[]{:S(2)}) copy-start(bf16[2048,1024]{1,0:T(8,128)(2,1)} %param.7) | copy-start | bytes 12582916
  154.3 111.5 %reduce-scatter.5.cloned.1.call-start = ((), (), s32[]{:S(2)}) async-start(), calls=%async_computation.3 | async-start | bytes 655360 | tf_op jit(solution)/shard_map/reduce_scatter | solution.py:39
Sparse Core Ops, SparseCore 0:
  154.4 87.4 reduce-scatter.2
  244.4 21.2 reduce-scatter.4
